TPU v7x, 32 devices: a whole 2x2x4 slice. The times are simulated.
32 devices in a mesh: seq: 8 (over y, x, core), dp: 4 (over z).
Axes of the slice: x: 2, y: 2, z: 4, core: 2. Of those that a mesh axis runs over, the one named last changes fastest.
Arguments:
- tokens: bfloat16 [4, 1024, 2048], P('dp', 'seq'), may hold values from -6 to 6
- valid_mask: int32 [4, 1024], P('dp', 'seq'), may hold values from 0 to 1, as said below
- teacher: bfloat16 [4, 1024, 2048], P('dp', 'seq'), may hold values from -6 to 6
- norm_one: bfloat16 [2048], P(('seq', 'dp')), may hold values from 0.5 to 1.5
- proj_gelu: bfloat16 [2048, 2560], P(('seq', 'dp')), may hold values from -0.125 to 0.125
- proj_rec: bfloat16 [2048, 2560], P(('seq', 'dp')), may hold values from -0.125 to 0.125
- conv_taps: bfloat16 [4, 2560], P(None, ('seq', 'dp')), may hold values from -3 to 3
- conv_bias: bfloat16 [2560], P(('seq', 'dp')), may hold values from -3 to 3
- gate_rec_w: bfloat16 [2560, 256], P(('seq', 'dp')), may hold values from -0.375 to 0.375
- gate_rec_b: bfloat16 [2560], P(('seq', 'dp')), may hold values from -4 to 4
- gate_inp_w: bfloat16 [2560, 256], P(('seq', 'dp')), may hold values from -0.375 to 0.375
- gate_inp_b: bfloat16 [2560], P(('seq', 'dp')), may hold values from -4 to 4
- rec_param: bfloat16 [2560], P(('seq', 'dp')), may hold values from 4 to 16
- proj_out: bfloat16 [2560, 2048], P(None, ('seq', 'dp')), may hold values from -0.25 to 0.25
- norm_two: bfloat16 [2048], P(('seq', 'dp')), may hold values from 0.5 to 1.5
- mlp_gate: bfloat16 [2048, 6144], P(('seq', 'dp')), may hold values from -0.125 to 0.125
- mlp_up: bfloat16 [2048, 6144], P(('seq', 'dp')), may hold values from -0.125 to 0.125
- mlp_down: bfloat16 [6144, 2048], P(None, ('seq', 'dp')), may hold values from -0.15625 to 0.15625
Outputs:
- output: bfloat16 [4, 1024, 2048], P('dp', 'seq')
- mean_loss: float32 [], replicated
- grad_tokens: bfloat16 [4, 1024, 2048], P('dp', 'seq')
- grad_norm_one: float32 [2048], P(('seq', 'dp'))
- grad_proj_gelu: float32 [2048, 2560], P(('seq', 'dp'))
- grad_proj_rec: float32 [2048, 2560], P(('seq', 'dp'))
- grad_conv_taps: float32 [4, 2560], P(None, ('seq', 'dp'))
- grad_conv_bias: float32 [2560], P(('seq', 'dp'))
- grad_gate_rec_w: float32 [2560, 256], P(('seq', 'dp'))
- grad_gate_rec_b: float32 [2560], P(('seq', 'dp'))
- grad_gate_inp_w: float32 [2560, 256], P(('seq', 'dp'))
- grad_gate_inp_b: float32 [2560], P(('seq', 'dp'))
- grad_rec_param: float32 [2560], P(('seq', 'dp'))
- grad_proj_out: float32 [2560, 2048], P(None, ('seq', 'dp'))
- grad_norm_two: float32 [2048], P(('seq', 'dp'))
- grad_mlp_gate: float32 [2048, 6144], P(('seq', 'dp'))
- grad_mlp_up: float32 [2048, 6144], P(('seq', 'dp'))
- grad_mlp_down: float32 [6144, 2048], P(None, ('seq', 'dp'))
Inputs may be any that keep to these rules, and one draw needn't show every extreme that they name: `valid_mask`: the last token of every sequence has 1.
All inputs are finite; a program needn't handle non-finite values.
Results may differ from a plain program's by a relative error of at most 0.0075.
Values may be sent and summed in bfloat16 or wider, within the bound.
A program may use at most 384 MiB of HBM per device.

v0:
```python
import jax
import jax.numpy as jnp
from jax import lax
from jax.sharding import PartitionSpec as P

NB = 10
BW = 256
CONV = 4
norm_eps = 1e-06
gate_power = 8.0
floor_square = 0.0001


def from_behind(value, axis, steps):
    count = lax.axis_size(axis)
    first, last = (max(0, -steps), min(count, count - steps))
    return lax.ppermute(value, axis, [(source, source + steps) for source in range(first, last)])


def rms_norm(values, gain_vec):
    return (
        values * lax.rsqrt(jnp.mean(values * values, axis=-1, keepdims=True) + norm_eps) * gain_vec
    )


def gate_terms(gate_rec, gate_inp, conv_val, rec_vals):
    recur_gate = jax.nn.sigmoid(gate_rec)
    admit_gate = jax.nn.sigmoid(gate_inp)
    log_decay = -gate_power * recur_gate * jax.nn.softplus(-rec_vals)
    decays = jnp.exp(log_decay)
    scaler = jnp.sqrt(jnp.maximum(-jnp.expm1(2.0 * log_decay), floor_square))
    return (decays, scaler * admit_gate * conv_val)


def compose(earlier, later_pair):
    return (earlier[0] * later_pair[0], later_pair[0] * earlier[1] + later_pair[1])


def contract_rows(left, right):
    return lax.dot_general(
        left, right, (((0,), (0,)), ((), ())), preferred_element_type=jnp.float32
    )


def times_trans(left, right):
    return lax.dot_general(
        left, right, (((1,), (1,)), ((), ())), preferred_element_type=jnp.float32
    )


def gelu_product(first, second):
    return jax.nn.gelu(first, approximate=True) * second


def on_device(
    tokens,
    valid_mask,
    teacher,
    norm_one,
    proj_gelu,
    proj_rec,
    conv_taps,
    conv_bias,
    gate_rec_w,
    gate_rec_b,
    gate_inp_w,
    gate_inp_b,
    rec_param,
    proj_out,
    norm_two,
    mlp_gate,
    mlp_up,
    mlp_down,
):
    full_w = (
        lax.all_gather(norm_one, ("seq", "dp"), axis=0, tiled=True),
        lax.all_gather(proj_gelu, ("seq", "dp"), axis=0, tiled=True),
        lax.all_gather(proj_rec, ("seq", "dp"), axis=0, tiled=True),
        lax.all_gather(conv_taps, ("seq", "dp"), axis=1, tiled=True),
        lax.all_gather(conv_bias, ("seq", "dp"), axis=0, tiled=True),
        lax.all_gather(gate_rec_w, ("seq", "dp"), axis=0, tiled=True),
        lax.all_gather(gate_rec_b, ("seq", "dp"), axis=0, tiled=True),
        lax.all_gather(gate_inp_w, ("seq", "dp"), axis=0, tiled=True),
        lax.all_gather(gate_inp_b, ("seq", "dp"), axis=0, tiled=True),
        lax.all_gather(rec_param, ("seq", "dp"), axis=0, tiled=True),
        lax.all_gather(proj_out, ("seq", "dp"), axis=1, tiled=True),
        lax.all_gather(norm_two, ("seq", "dp"), axis=0, tiled=True),
        lax.all_gather(mlp_gate, ("seq", "dp"), axis=0, tiled=True),
        lax.all_gather(mlp_up, ("seq", "dp"), axis=0, tiled=True),
        lax.all_gather(mlp_down, ("seq", "dp"), axis=1, tiled=True),
    )
    seq_count, local_len, model_width = tokens.shape
    row_count = seq_count * local_len
    rec_width = full_w[2].shape[1]
    fp32 = jnp.float32
    half = jnp.bfloat16
    flat_in = tokens.reshape(row_count, model_width).astype(fp32)
    gain_one = full_w[0].astype(fp32)
    normed_low = rms_norm(flat_in, gain_one).astype(half)
    gelu_pre = jnp.dot(normed_low, full_w[1], preferred_element_type=fp32)
    rec_pre = jnp.dot(normed_low, full_w[2], preferred_element_type=fp32)
    rec_seq = rec_pre.reshape(seq_count, local_len, rec_width)
    prev_edge = from_behind(rec_seq[:, local_len - (CONV - 1) :, :], "seq", 1)
    padded = jnp.concatenate([prev_edge, rec_seq], axis=1)
    tap_vals = full_w[3].astype(fp32)
    conv_sum = full_w[4].astype(fp32) + jnp.zeros_like(rec_seq)
    for offset in range(CONV):
        conv_sum = (
            conv_sum
            + tap_vals[offset] * padded[:, CONV - 1 - offset : CONV - 1 - offset + local_len]
        )
    conv_low = conv_sum.astype(half)
    conv_val = conv_low.astype(fp32)
    blocks = conv_low.reshape(row_count, NB, BW)
    rec_mat = full_w[5].reshape(NB, BW, BW)
    inp_mat = full_w[7].reshape(NB, BW, BW)
    gate_rec = jnp.einsum("tki,kij->tkj", blocks, rec_mat, preferred_element_type=fp32).reshape(
        seq_count, local_len, rec_width
    ) + full_w[6].astype(fp32)
    gate_inp = jnp.einsum("tki,kij->tkj", blocks, inp_mat, preferred_element_type=fp32).reshape(
        seq_count, local_len, rec_width
    ) + full_w[8].astype(fp32)
    rec_vals = full_w[9].astype(fp32)
    decays, drives = gate_terms(gate_rec, gate_inp, conv_val, rec_vals)
    cum_decay, local_state = lax.associative_scan(compose, (decays, drives), axis=1)
    total_decay = cum_decay[:, -1]
    total_state = local_state[:, -1]

    def forward_turn(turn_index, incoming):
        return from_behind(total_decay * incoming + total_state, "seq", 1)

    entering = lax.fori_loop(0, lax.axis_size("seq") - 1, forward_turn, jnp.zeros_like(total_state))
    states = local_state + cum_decay * entering[:, None, :]
    flat_states = states.reshape(row_count, rec_width)
    mixed_low = gelu_product(gelu_pre, flat_states).astype(half)
    middle = flat_in + jnp.dot(mixed_low, full_w[10], preferred_element_type=fp32)
    gain_two = full_w[11].astype(fp32)
    normed_two_low = rms_norm(middle, gain_two).astype(half)
    gate_pre = jnp.dot(normed_two_low, full_w[12], preferred_element_type=fp32)
    up_pre = jnp.dot(normed_two_low, full_w[13], preferred_element_type=fp32)
    hidden_low = gelu_product(gate_pre, up_pre).astype(half)
    result = middle + jnp.dot(hidden_low, full_w[14], preferred_element_type=fp32)
    target = teacher.reshape(row_count, model_width).astype(fp32)
    differ = result - target
    mask_val = valid_mask.reshape(row_count).astype(fp32)
    totals = lax.psum(
        (jnp.sum(mask_val), 0.5 * jnp.sum(mask_val[:, None] * differ * differ)), ("seq", "dp")
    )
    token_total = row_count * lax.axis_size("seq") * lax.axis_size("dp")
    mean_loss = totals[1] / (totals[0] * model_width)
    back_w = (
        lax.all_gather(norm_one, ("seq", "dp"), axis=0, tiled=True),
        lax.all_gather(proj_gelu, ("seq", "dp"), axis=0, tiled=True),
        lax.all_gather(proj_rec, ("seq", "dp"), axis=0, tiled=True),
        lax.all_gather(conv_taps, ("seq", "dp"), axis=1, tiled=True),
        lax.all_gather(conv_bias, ("seq", "dp"), axis=0, tiled=True),
        lax.all_gather(gate_rec_w, ("seq", "dp"), axis=0, tiled=True),
        lax.all_gather(gate_rec_b, ("seq", "dp"), axis=0, tiled=True),
        lax.all_gather(gate_inp_w, ("seq", "dp"), axis=0, tiled=True),
        lax.all_gather(gate_inp_b, ("seq", "dp"), axis=0, tiled=True),
        lax.all_gather(rec_param, ("seq", "dp"), axis=0, tiled=True),
        lax.all_gather(proj_out, ("seq", "dp"), axis=1, tiled=True),
        lax.all_gather(norm_two, ("seq", "dp"), axis=0, tiled=True),
        lax.all_gather(mlp_gate, ("seq", "dp"), axis=0, tiled=True),
        lax.all_gather(mlp_up, ("seq", "dp"), axis=0, tiled=True),
        lax.all_gather(mlp_down, ("seq", "dp"), axis=1, tiled=True),
    )
    grad_result = mask_val[:, None] * (token_total / totals[0]) * differ
    down_low = grad_result.astype(half)
    grad_mlp_down = contract_rows(hidden_low, down_low)
    grad_hidden = times_trans(down_low, back_w[14])
    _, pull_mlp = jax.vjp(gelu_product, gate_pre, up_pre)
    grad_gate_pre, grad_up_pre = pull_mlp(grad_hidden)
    gate_low = grad_gate_pre.astype(half)
    up_low = grad_up_pre.astype(half)
    grad_mlp_gate = contract_rows(normed_two_low, gate_low)
    grad_mlp_up = contract_rows(normed_two_low, up_low)
    grad_normed_two = times_trans(gate_low, back_w[12]) + times_trans(up_low, back_w[13])
    _, pull_norm_two = jax.vjp(rms_norm, middle, gain_two)
    grad_middle_norm, grad_norm_two = pull_norm_two(grad_normed_two)
    grad_middle = grad_result + grad_middle_norm
    middle_low = grad_middle.astype(half)
    grad_proj_out = contract_rows(mixed_low, middle_low)
    grad_mixed = times_trans(middle_low, back_w[10])
    _, pull_mix = jax.vjp(gelu_product, gelu_pre, flat_states)
    grad_gelu_pre, grad_states = pull_mix(grad_mixed)
    grad_states = grad_states.reshape(seq_count, local_len, rec_width)
    later_decay = jnp.concatenate([decays[:, 1:], jnp.ones_like(decays[:, :1])], axis=1)
    tail_decay, local_adj = lax.associative_scan(
        compose, (later_decay, grad_states), reverse=True, axis=1
    )
    head_term = decays[:, 0] * local_adj[:, 0]

    def backward_turn(turn_index, incoming):
        return from_behind(total_decay * incoming + head_term, "seq", -1)

    leaving = lax.fori_loop(0, lax.axis_size("seq") - 1, backward_turn, jnp.zeros_like(head_term))
    adjoint = local_adj + tail_decay * leaving[:, None, :]
    prior_state = jnp.concatenate([entering[:, None, :], states[:, :-1]], axis=1)
    _, pull_gates = jax.vjp(gate_terms, gate_rec, gate_inp, conv_val, rec_vals)
    grad_rec_gate, grad_inp_gate, grad_conv_direct, grad_rec_param = pull_gates(
        (adjoint * prior_state, adjoint)
    )
    rec_gate_low = grad_rec_gate.astype(half).reshape(row_count, NB, BW)
    inp_gate_low = grad_inp_gate.astype(half).reshape(row_count, NB, BW)
    grad_gate_rec_b = jnp.sum(rec_gate_low.reshape(row_count, rec_width).astype(fp32), axis=0)
    grad_gate_inp_b = jnp.sum(inp_gate_low.reshape(row_count, rec_width).astype(fp32), axis=0)
    grad_gate_rec_w = jnp.einsum(
        "tki,tkj->kij", blocks, rec_gate_low, preferred_element_type=fp32
    ).reshape(rec_width, BW)
    grad_gate_inp_w = jnp.einsum(
        "tki,tkj->kij", blocks, inp_gate_low, preferred_element_type=fp32
    ).reshape(rec_width, BW)
    back_rec_mat = back_w[5].reshape(NB, BW, BW)
    back_inp_mat = back_w[7].reshape(NB, BW, BW)
    gate_back = jnp.einsum(
        "tkj,kij->tki", rec_gate_low, back_rec_mat, preferred_element_type=fp32
    ) + jnp.einsum("tkj,kij->tki", inp_gate_low, back_inp_mat, preferred_element_type=fp32)
    grad_conv = grad_conv_direct + gate_back.reshape(seq_count, local_len, rec_width)
    grad_conv_bias = jnp.sum(grad_conv, axis=(0, 1))
    back_taps = back_w[3].astype(fp32)
    tap_grads = []
    grad_padded = jnp.zeros((seq_count, local_len + CONV - 1, rec_width), fp32)
    for offset in range(CONV):
        window = padded[:, CONV - 1 - offset : CONV - 1 - offset + local_len]
        tap_grads.append(jnp.sum(grad_conv * window, axis=(0, 1)))
        grad_padded = grad_padded + jnp.pad(
            back_taps[offset] * grad_conv, ((0, 0), (CONV - 1 - offset, offset), (0, 0))
        )
    grad_conv_taps = jnp.stack(tap_grads, axis=0)
    from_next = from_behind(grad_padded[:, : CONV - 1], "seq", -1)
    grad_rec_seq = grad_padded[:, CONV - 1 :] + jnp.pad(
        from_next, ((0, 0), (local_len - (CONV - 1), 0), (0, 0))
    )
    rec_back_low = grad_rec_seq.reshape(row_count, rec_width).astype(half)
    gelu_low = grad_gelu_pre.astype(half)
    grad_proj_rec = contract_rows(normed_low, rec_back_low)
    grad_proj_gelu = contract_rows(normed_low, gelu_low)
    grad_normed = times_trans(rec_back_low, back_w[2]) + times_trans(gelu_low, back_w[1])
    _, pull_norm_one = jax.vjp(rms_norm, flat_in, back_w[0].astype(fp32))
    grad_in_norm, grad_norm_one = pull_norm_one(grad_normed)
    grad_tokens = (grad_middle + grad_in_norm).reshape(tokens.shape).astype(half)
    summed = (
        lax.psum_scatter(grad_norm_one, ("seq", "dp"), scatter_dimension=0, tiled=True),
        lax.psum_scatter(grad_proj_gelu, ("seq", "dp"), scatter_dimension=0, tiled=True),
        lax.psum_scatter(grad_proj_rec, ("seq", "dp"), scatter_dimension=0, tiled=True),
        lax.psum_scatter(grad_conv_taps, ("seq", "dp"), scatter_dimension=1, tiled=True),
        lax.psum_scatter(grad_conv_bias, ("seq", "dp"), scatter_dimension=0, tiled=True),
        lax.psum_scatter(grad_gate_rec_w, ("seq", "dp"), scatter_dimension=0, tiled=True),
        lax.psum_scatter(grad_gate_rec_b, ("seq", "dp"), scatter_dimension=0, tiled=True),
        lax.psum_scatter(grad_gate_inp_w, ("seq", "dp"), scatter_dimension=0, tiled=True),
        lax.psum_scatter(grad_gate_inp_b, ("seq", "dp"), scatter_dimension=0, tiled=True),
        lax.psum_scatter(grad_rec_param, ("seq", "dp"), scatter_dimension=0, tiled=True),
        lax.psum_scatter(grad_proj_out, ("seq", "dp"), scatter_dimension=1, tiled=True),
        lax.psum_scatter(grad_norm_two, ("seq", "dp"), scatter_dimension=0, tiled=True),
        lax.psum_scatter(grad_mlp_gate, ("seq", "dp"), scatter_dimension=0, tiled=True),
        lax.psum_scatter(grad_mlp_up, ("seq", "dp"), scatter_dimension=0, tiled=True),
        lax.psum_scatter(grad_mlp_down, ("seq", "dp"), scatter_dimension=1, tiled=True),
    )
    output = result.reshape(tokens.shape).astype(half)
    return (
        output,
        mean_loss,
        grad_tokens,
        summed[0],
        summed[1],
        summed[2],
        summed[3],
        summed[4],
        summed[5],
        summed[6],
        summed[7],
        summed[8],
        summed[9],
        summed[10],
        summed[11],
        summed[12],
        summed[13],
        summed[14],
    )


def solution(mesh):
    in_specs = (
        P("dp", "seq", None),
        P("dp", "seq"),
        P("dp", "seq", None),
        P(("seq", "dp")),
        P(("seq", "dp"), None),
        P(("seq", "dp"), None),
        P(None, ("seq", "dp")),
        P(("seq", "dp")),
        P(("seq", "dp"), None),
        P(("seq", "dp")),
        P(("seq", "dp"), None),
        P(("seq", "dp")),
        P(("seq", "dp")),
        P(None, ("seq", "dp")),
        P(("seq", "dp")),
        P(("seq", "dp"), None),
        P(("seq", "dp"), None),
        P(None, ("seq", "dp")),
    )
    out_specs = (
        P("dp", "seq", None),
        P(),
        P("dp", "seq", None),
        P(("seq", "dp")),
        P(("seq", "dp"), None),
        P(("seq", "dp"), None),
        P(None, ("seq", "dp")),
        P(("seq", "dp")),
        P(("seq", "dp"), None),
        P(("seq", "dp")),
        P(("seq", "dp"), None),
        P(("seq", "dp")),
        P(("seq", "dp")),
        P(None, ("seq", "dp")),
        P(("seq", "dp")),
        P(("seq", "dp"), None),
        P(("seq", "dp"), None),
        P(None, ("seq", "dp")),
    )
    return jax.shard_map(
        on_device, mesh=mesh, in_specs=in_specs, out_specs=out_specs, check_vma=False
    )
```

profile of v0, /device:TPU:0, one launch (start us, length us, event | category | flops | bytes accessed | tf_op | source)
XLA Modules:
  0.0 4295.3 jit_solution(4317977598982749582)
XLA Ops:
  13.4 43.0 %psum.15 = f32[]{:T(128)} all-reduce(f32[]{:T(128)} %convert_reduce_fusion.2), channel_id=1, replica_groups=mesh['seq'=8,'dp'=4] {'seq','dp'}, use_global_device_ids=true, to_apply=%region_7.8 | all-reduce | flops 1 | bytes 8 | tf_op jit(solution)/shard_map/psum | solution.py:146
  57.9 42.2 all-reduce.76
  100.1 65.6 %all-gather = bf16[32,80,4]{1,2,0:T(4,128)(2,1)S(1)} all-gather(bf16[1,80,4]{1,2,0:T(4,128)(2,1)S(1)} %bitcast.182), channel_id=1, replica_groups=mesh['seq'=8,'dp'=4] {'seq','dp'}, dimensions={0}, use_global_device_ids=true | all-gather | bytes 21120 | tf_op jit(solution)/shard_map/all_gather | solution.py:79
  184.8 28.6 all-gather.16.cloned.1.call-done
  335.3 10.0 slice.546
  345.3 9.9 slice.539
  431.4 32.8 while.20
  483.3 63.1 %all-gather.20.cloned.1.call-done = bf16[2048,6144]{1,0:T(8,128)(2,1)} async-done(((bf16[64,6144]{1,0:T(8,128)(2,1)}), bf16[2048,6144]{1,0:T(8,128)(2,1)}) %all-gather.20.cloned.1.call-update) | async-done | bytes 25165840 | tf_op jit(solution)/shard_map/all_gather | solution.py:88
  546.4 13.4 fusion.106
  559.8 142.1 %all-gather.22.cloned.1.call-done = bf16[2048,6144]{1,0:T(8,128)(2,1)} async-done(((bf16[64,6144]{1,0:T(8,128)(2,1)}), bf16[2048,6144]{1,0:T(8,128)(2,1)}) %all-gather.22.cloned.1.call-update) | async-done | bytes 25165840 | tf_op jit(solution)/shard_map/all_gather | solution.py:89
  701.9 15.9 multiply_convert_fusion.1
  717.8 139.8 %all-gather.24.cloned.1.call-done = bf16[6144,2048]{0,1:T(8,128)(2,1)} async-done(((bf16[6144,64]{0,1:T(8,128)(2,1)}), bf16[6144,2048]{0,1:T(8,128)(2,1)}) %all-gather.24.cloned.1.call-update) | async-done | bytes 25165840 | tf_op jit(solution)/shard_map/all_gather | solution.py:90
  857.6 15.0 multiply_convert_fusion.3
  872.6 14.6 multiply_convert_fusion
  887.2 14.4 fusion.107
  901.6 16.1 multiply_reduce_fusion.5
  930.2 10.8 reverse.8
  1088.8 33.9 while.21
  1137.5 10.8 rev.12
  1148.2 10.9 rev.11
  1235.0 20.5 fusion.114
  1256.5 20.9 fusion.112
  1277.7 20.9 fusion.113
  1316.2 47.7 %all-reduce.75 = (f32[]{:T(128)}, f32[2048]{0:T(1024)S(1)}, f32[2560]{0:T(1024)S(1)}, f32[2560]{0:T(1024)S(1)}, f32[2560]{0:T(1024)S(1)}, /*index=5*/f32[2560]{0:T(1024)S(1)}, f32[2048]{0:T(1024)S(1)}) all-reduce(f32[]{:T(128)S(6)} %mul.797, f32[2048]{0:T(1024)S(1)} %get-tuple-element.69, ...), channel_id=1, replica_groups=mesh['seq'=8,'dp'=4] {'seq','dp'}, use_global_device_ids=true, to_apply=%region_5.6 | all-reduce | flops 14337 | bytes 114696 | tf_op jit(solution)/shard_map/psum | solution.py:146
  1371.9 101.6 %reduce-scatter.16.cloned.1.call-done = f32[80,256]{1,0:T(8,128)} async-done(((f32[2560,256]{1,0:T(8,128)}), f32[80,256]{1,0:T(8,128)}) %reduce-scatter.16.cloned.1.call-update) | async-done | bytes 81936 | tf_op jit(solution)/shard_map/reduce_scatter | solution.py:249
  1473.6 141.3 %reduce-scatter.18.cloned.1.call-done = f32[80,256]{1,0:T(8,128)} async-done(((f32[2560,256]{1,0:T(8,128)}), f32[80,256]{1,0:T(8,128)}) %reduce-scatter.18.cloned.1.call-update) | async-done | bytes 81936 | tf_op jit(solution)/shard_map/reduce_scatter | solution.py:251
  1614.9 452.1 %reduce-scatter.20.cloned.1.call-done = f32[2560,64]{0,1:T(8,128)} async-done(((f32[2560,2048]{0,1:T(8,128)}), f32[2560,64]{0,1:T(8,128)}) %reduce-scatter.20.cloned.1.call-update) | async-done | bytes 655376 | tf_op jit(solution)/shard_map/reduce_scatter | solution.py:254
  2067.0 452.5 %reduce-scatter.12.cloned.1.call-done = f32[64,2560]{1,0:T(8,128)} async-done(((f32[2048,2560]{1,0:T(8,128)}), f32[64,2560]{1,0:T(8,128)}) %reduce-scatter.12.cloned.1.call-update) | async-done | bytes 655376 | tf_op jit(solution)/shard_map/reduce_scatter | solution.py:245
  2519.5 452.3 %reduce-scatter.14.cloned.1.call-done = f32[64,2560]{1,0:T(8,128)} async-done(((f32[2048,2560]{1,0:T(8,128)}), f32[64,2560]{1,0:T(8,128)}) %reduce-scatter.14.cloned.1.call-update) | async-done | bytes 655376 | tf_op jit(solution)/shard_map/reduce_scatter | solution.py:246
  2971.8 438.4 %reduce-scatter.26.cloned.1.call-done = f32[6144,64]{0,1:T(8,128)} async-done(((f32[6144,2048]{0,1:T(8,128)}), f32[6144,64]{0,1:T(8,128)}) %reduce-scatter.26.cloned.1.call-update) | async-done | bytes 1572880 | tf_op jit(solution)/shard_map/reduce_scatter | solution.py:258
  3410.2 438.6 %reduce-scatter.22.cloned.1.call-done = f32[64,6144]{1,0:T(8,128)} async-done(((f32[2048,6144]{1,0:T(8,128)}), f32[64,6144]{1,0:T(8,128)}) %reduce-scatter.22.cloned.1.call-update) | async-done | bytes 1572880 | tf_op jit(solution)/shard_map/reduce_scatter | solution.py:256
  3848.8 438.6 %reduce-scatter.24.cloned.1.call-done = f32[64,6144]{1,0:T(8,128)} async-done(((f32[2048,6144]{1,0:T(8,128)}), f32[64,6144]{1,0:T(8,128)}) %reduce-scatter.24.cloned.1.call-update) | async-done | bytes 1572880 | tf_op jit(solution)/shard_map/reduce_scatter | solution.py:257
  (585 shorter events, 584.1 us)
Async XLA Ops:
  7.2 160.6 %all-gather.12.cloned.1.call-start = ((), (), s32[]{:S(2)}) async-start(), calls=%async_computation.10 | async-start | bytes 10813440 | tf_op jit(solution)/shard_map/all_gather | solution.py:78
  7.9 169.3 %all-gather.14.cloned.1.call-start = ((), (), s32[]{:S(2)}) async-start(), calls=%async_computation.11 | async-start | bytes 1351680 | tf_op jit(solution)/shard_map/all_gather | solution.py:81
  8.7 204.7 %all-gather.16.cloned.1.call-start = ((), (), s32[]{:S(2)}) async-start(), calls=%async_computation.12 | async-start | bytes 1351680 | tf_op jit(solution)/shard_map/all_gather | solution.py:83
  9.4 454.9 %all-gather.10.cloned.1.call-start = ((), (), s32[]{:S(2)}) async-start(), calls=%async_computation.9 | async-start | bytes 10813440 | tf_op jit(solution)/shard_map/all_gather | solution.py:77
  10.1 463.5 %all-gather.18.cloned.1.call-start = ((), (), s32[]{:S(2)}) async-start(), calls=%async_computation.13 | async-start | bytes 10813440 | tf_op jit(solution)/shard_map/all_gather | solution.py:86
  10.7 535.7 %all-gather.20.cloned.1.call-start = ((), (), s32[]{:S(2)}) async-start(), calls=%async_computation.14 | async-start | bytes 25952256 | tf_op jit(solution)/shard_map/all_gather | solution.py:88
  11.2 690.6 %all-gather.22.cloned.1.call-start = ((), (), s32[]{:S(2)}) async-start(), calls=%async_computation.15 | async-start | bytes 25952256 | tf_op jit(solution)/shard_map/all_gather | solution.py:89
  12.0 845.6 %all-gather.24.cloned.1.call-start = ((), (), s32[]{:S(2)}) async-start(), calls=%async_computation.16 | async-start | bytes 25952256 | tf_op jit(solution)/shard_map/all_gather | solution.py:90
  12.7 1357.7 %reduce-scatter.28.cloned.1.call-start = ((), (), s32[]{:S(2)}) async-start(), calls=%async_computation.25 | async-start | bytes 1351680
  431.5 3.1 collective-permute-start
  434.6 3.8 collective-permute-start
  438.5 5.2 collective-permute-start
  443.7 5.2 collective-permute-start
  448.9 5.2 collective-permute-start
  454.1 5.0 collective-permute-start
  459.1 5.0 collective-permute-start
  1088.8 3.1 collective-permute-start.1
  1091.9 4.8 collective-permute-start.1
  1096.7 5.0 collective-permute-start.1
  1101.7 5.0 collective-permute-start.1
  1106.7 5.0 collective-permute-start.1
  1111.7 5.1 collective-permute-start.1
  1116.8 5.9 collective-permute-start.1
  1191.8 281.8 %reduce-scatter.16.cloned.1.call-start = ((), (), s32[]{:S(2)}) async-start(), calls=%async_computation.19 | async-start | bytes 2703360 | tf_op jit(solution)/shard_map/reduce_scatter | solution.py:249
  1193.8 421.0 %reduce-scatter.18.cloned.1.call-start = ((), (), s32[]{:S(2)}) async-start(), calls=%async_computation.20 | async-start | bytes 2703360 | tf_op jit(solution)/shard_map/reduce_scatter | solution.py:251
  1196.9 870.1 %reduce-scatter.20.cloned.1.call-start = ((), (), s32[]{:S(2)}) async-start(), calls=%async_computation.21 | async-start | bytes 21626880 | tf_op jit(solution)/shard_map/reduce_scatter | solution.py:254
  1207.0 1312.5 %reduce-scatter.12.cloned.1.call-start = ((), (), s32[]{:S(2)}) async-start(), calls=%async_computation.17 | async-start | bytes 21626880 | tf_op jit(solution)/shard_map/reduce_scatter | solution.py:245
  1216.8 1755.0 %reduce-scatter.14.cloned.1.call-start = ((), (), s32[]{:S(2)}) async-start(), calls=%async_computation.18 | async-start | bytes 21626880 | tf_op jit(solution)/shard_map/reduce_scatter | solution.py:246
  1218.8 5.9 collective-permute-start.3
  1233.6 2176.6 %reduce-scatter.26.cloned.1.call-start = ((), (), s32[]{:S(2)}) async-start(), calls=%async_computation.24 | async-start | bytes 51904512 | tf_op jit(solution)/shard_map/reduce_scatter | solution.py:258
  1255.5 2593.3 %reduce-scatter.22.cloned.1.call-start = ((), (), s32[]{:S(2)}) async-start(), calls=%async_computation.22 | async-start | bytes 51904512 | tf_op jit(solution)/shard_map/reduce_scatter | solution.py:256
  1277.4 3010.0 %reduce-scatter.24.cloned.1.call-start = ((), (), s32[]{:S(2)}) async-start(), calls=%async_computation.23 | async-start | bytes 51904512 | tf_op jit(solution)/shard_map/reduce_scatter | solution.py:257
  (102 other events, 1568.7 us)
Sparse Core Ops, SparseCore 0:
  10.9 90.3 all-gather.11
  104.1 53.0 all-gather.13
  160.1 53.2 all-gather.15
  216.0 85.7 all-gather.9
  304.5 85.2 all-gather.17
  392.6 153.6 all-gather.19
  549.2 152.6 all-gather.21
  704.8 152.8 all-gather.23
  1191.9 141.6 reduce-scatter.27
  1336.4 137.1 reduce-scatter.15
  1476.5 138.2 reduce-scatter.17
  1617.7 449.2 reduce-scatter.19
  2070.0 449.4 reduce-scatter.11
  2522.3 449.4 reduce-scatter.13
  2979.8 430.3 reduce-scatter.25
  3418.2 430.5 reduce-scatter.21
  3856.8 430.5 reduce-scatter.23
where the time goes:
time: 4310 us; the launch traced here: 4300 us
  waiting for transfers between devices  3330 us (77%)
  local copies, waits for them, and re-layouts  348 us (8%)
  matrix products  241 us (6%)
  blocking collectives  198 us (5%)
  other arithmetic  119 us (3%)
    reduce_scatter x1, waiting for transfers between devices, on_device(): lax.psum_scatter(grad_proj_gelu, ('seq', 'dp'), scatter_dimension=0, tile...  452 us
    reduce_scatter x1, waiting for transfers between devices, on_device(): lax.psum_scatter(grad_proj_rec, ('seq', 'dp'), scatter_dimension=0, tiled...  452 us
    reduce_scatter x1, waiting for transfers between devices, on_device(): lax.psum_scatter(grad_proj_out, ('seq', 'dp'), scatter_dimension=1, tiled...  452 us
    reduce_scatter x1, waiting for transfers between devices, on_device(): lax.psum_scatter(grad_mlp_up, ('seq', 'dp'), scatter_dimension=0, tiled=T...  439 us
    reduce_scatter x1, waiting for transfers between devices, on_device(): lax.psum_scatter(grad_mlp_gate, ('seq', 'dp'), scatter_dimension=0, tiled...  439 us
    reduce_scatter x1, waiting for transfers between devices, on_device(): lax.psum_scatter(grad_mlp_down, ('seq', 'dp'), scatter_dimension=1, tiled...  438 us
    all_gather x1, waiting for transfers between devices, on_device(): lax.all_gather(mlp_up, ('seq', 'dp'), axis=0, tiled=True)  142 us
    reduce_scatter x1, waiting for transfers between devices, on_device(): lax.psum_scatter(grad_gate_inp_w, ('seq', 'dp'), scatter_dimension=0, til...  141 us
  transfers between devices with their start and end apart: 33, of which 28 were waited for; matrix products, arithmetic and copies ran while one was open for 9% of the time, Pallas kernels for 0%

commit v1 on v0

--- a/solution.py
+++ b/solution.py
@@ -144,7 +144,8 @@
     differ = result - target
     mask_val = valid_mask.reshape(row_count).astype(fp32)
     totals = lax.psum(
-        (jnp.sum(mask_val), 0.5 * jnp.sum(mask_val[:, None] * differ * differ)), ("seq", "dp")
+        lax.psum((jnp.sum(mask_val), 0.5 * jnp.sum(mask_val[:, None] * differ * differ)), "dp"),
+        "seq",
     )
     token_total = row_count * lax.axis_size("seq") * lax.axis_size("dp")
     mean_loss = totals[1] / (totals[0] * model_width)

time: 4310 us -> 4350 us (level)
  waiting for transfers between devices: 3330 us -> 3380 us
    psum x2 -> x1, blocking collectives: 90.7 us -> 10.4 us  [on_device(): lax.psum((jnp.sum(mask_val), 0.5 * jnp.sum(mask_val[:, None] * differ * d...]
    unnamed x1 -> x2, blocking collectives: 42.2 us -> 90.6 us
where the time goes in v1:
time: 4350 us; the launch traced here: 4330 us
  waiting for transfers between devices  3380 us (78%)
  local copies, waits for them, and re-layouts  348 us (8%)
  matrix products  241 us (6%)
  blocking collectives  180 us (4%)
  other arithmetic  120 us (3%)
    reduce_scatter x1, waiting for transfers between devices, on_device(): lax.psum_scatter(grad_proj_gelu, ('seq', 'dp'), scatter_dimension=0, tile...  452 us
    reduce_scatter x1, waiting for transfers between devices, on_device(): lax.psum_scatter(grad_proj_rec, ('seq', 'dp'), scatter_dimension=0, tiled...  452 us
    reduce_scatter x1, waiting for transfers between devices, on_device(): lax.psum_scatter(grad_proj_out, ('seq', 'dp'), scatter_dimension=1, tiled...  452 us
    reduce_scatter x1, waiting for transfers between devices, on_device(): lax.psum_scatter(grad_mlp_up, ('seq', 'dp'), scatter_dimension=0, tiled=T...  439 us
    reduce_scatter x1, waiting for transfers between devices, on_device(): lax.psum_scatter(grad_mlp_gate, ('seq', 'dp'), scatter_dimension=0, tiled...  438 us
    reduce_scatter x1, waiting for transfers between devices, on_device(): lax.psum_scatter(grad_mlp_down, ('seq', 'dp'), scatter_dimension=1, tiled...  438 us
    all_gather x1, waiting for transfers between devices, on_device(): lax.all_gather(mlp_up, ('seq', 'dp'), axis=0, tiled=True)  142 us
    reduce_scatter x1, waiting for transfers between devices, on_device(): lax.psum_scatter(grad_gate_inp_w, ('seq', 'dp'), scatter_dimension=0, til...  141 us
  transfers between devices with their start and end apart: 33, of which 28 were waited for; matrix products, arithmetic and copies ran while one was open for 9% of the time, Pallas kernels for 0%

profile of v1, /device:TPU:0, one launch (start us, length us, event | category | flops | bytes accessed | tf_op | source)
XLA Modules:
  0.0 4328.7 jit_solution(9460449027515651214)
XLA Ops:
  14.3 43.2 all-reduce.78
  57.5 66.3 %all-gather = bf16[32,80,4]{1,2,0:T(4,128)(2,1)S(1)} all-gather(bf16[1,80,4]{1,2,0:T(4,128)(2,1)S(1)} %bitcast.182), channel_id=1, replica_groups=mesh['seq'=8,'dp'=4] {'seq','dp'}, dimensions={0}, use_global_device_ids=true | all-gather | bytes 21120 | tf_op jit(solution)/shard_map/all_gather | solution.py:79
  134.7 21.8 all-gather.14.cloned.1.call-done
  163.7 48.9 %all-gather.16.cloned.1.call-done = bf16[2560,256]{1,0:T(8,128)(2,1)} async-done(((bf16[80,256]{1,0:T(8,128)(2,1)}), bf16[2560,256]{1,0:T(8,128)(2,1)}) %all-gather.16.cloned.1.call-update) | async-done | bytes 1310736 | tf_op jit(solution)/shard_map/all_gather | solution.py:83
  420.6 33.1 while.20
  472.6 72.9 %all-gather.20.cloned.1.call-done = bf16[2048,6144]{1,0:T(8,128)(2,1)} async-done(((bf16[64,6144]{1,0:T(8,128)(2,1)}), bf16[2048,6144]{1,0:T(8,128)(2,1)}) %all-gather.20.cloned.1.call-update) | async-done | bytes 25165840 | tf_op jit(solution)/shard_map/all_gather | solution.py:88
  545.5 13.4 fusion.106
  559.0 142.3 %all-gather.22.cloned.1.call-done = bf16[2048,6144]{1,0:T(8,128)(2,1)} async-done(((bf16[64,6144]{1,0:T(8,128)(2,1)}), bf16[2048,6144]{1,0:T(8,128)(2,1)}) %all-gather.22.cloned.1.call-update) | async-done | bytes 25165840 | tf_op jit(solution)/shard_map/all_gather | solution.py:89
  701.3 15.9 multiply_convert_fusion.1
  717.2 139.8 %all-gather.24.cloned.1.call-done = bf16[6144,2048]{0,1:T(8,128)(2,1)} async-done(((bf16[6144,64]{0,1:T(8,128)(2,1)}), bf16[6144,2048]{0,1:T(8,128)(2,1)}) %all-gather.24.cloned.1.call-update) | async-done | bytes 25165840 | tf_op jit(solution)/shard_map/all_gather | solution.py:90
  857.0 15.4 fusion.42
  882.9 10.4 all-reduce.77
  893.3 12.8 all-reduce.76
  908.3 15.0 multiply_convert_fusion
  923.3 14.4 fusion.107
  937.7 15.7 multiply_reduce_fusion.5
  965.1 10.8 reverse.8
  1123.9 32.7 while.21
  1171.3 10.8 rev.12
  1182.0 10.8 rev.11
  1268.6 20.5 fusion.114
  1290.1 20.9 fusion.112
  1311.3 20.9 fusion.113
  1349.8 47.5 %all-reduce.75 = (f32[2048]{0:T(1024)S(1)}, f32[2560]{0:T(1024)S(1)}, f32[2560]{0:T(1024)S(1)}, f32[2560]{0:T(1024)S(1)}, f32[2560]{0:T(1024)S(1)}, /*index=5*/f32[2048]{0:T(1024)S(1)}) all-reduce(f32[2048]{0:T(1024)S(1)} %get-tuple-element.69, f32[2560]{0:T(1024)S(1)} %copy-done.71, ...), channel_id=2, replica_groups=mesh['seq'=8,'dp'=4] {'seq','dp'}, use_global_device_ids=true, to_apply=%region_15.16.clone | all-reduce | flops 14336 | bytes 114688
  1404.6 102.4 %reduce-scatter.16.cloned.1.call-done = f32[80,256]{1,0:T(8,128)} async-done(((f32[2560,256]{1,0:T(8,128)}), f32[80,256]{1,0:T(8,128)}) %reduce-scatter.16.cloned.1.call-update) | async-done | bytes 81936 | tf_op jit(solution)/shard_map/reduce_scatter | solution.py:250
  1507.0 141.4 %reduce-scatter.18.cloned.1.call-done = f32[80,256]{1,0:T(8,128)} async-done(((f32[2560,256]{1,0:T(8,128)}), f32[80,256]{1,0:T(8,128)}) %reduce-scatter.18.cloned.1.call-update) | async-done | bytes 81936 | tf_op jit(solution)/shard_map/reduce_scatter | solution.py:252
  1648.5 451.8 %reduce-scatter.20.cloned.1.call-done = f32[2560,64]{0,1:T(8,128)} async-done(((f32[2560,2048]{0,1:T(8,128)}), f32[2560,64]{0,1:T(8,128)}) %reduce-scatter.20.cloned.1.call-update) | async-done | bytes 655376 | tf_op jit(solution)/shard_map/reduce_scatter | solution.py:255
  2100.3 452.5 %reduce-scatter.12.cloned.1.call-done = f32[64,2560]{1,0:T(8,128)} async-done(((f32[2048,2560]{1,0:T(8,128)}), f32[64,2560]{1,0:T(8,128)}) %reduce-scatter.12.cloned.1.call-update) | async-done | bytes 655376 | tf_op jit(solution)/shard_map/reduce_scatter | solution.py:246
  2552.7 452.3 %reduce-scatter.14.cloned.1.call-done = f32[64,2560]{1,0:T(8,128)} async-done(((f32[2048,2560]{1,0:T(8,128)}), f32[64,2560]{1,0:T(8,128)}) %reduce-scatter.14.cloned.1.call-update) | async-done | bytes 655376 | tf_op jit(solution)/shard_map/reduce_scatter | solution.py:247
  3005.1 438.4 %reduce-scatter.26.cloned.1.call-done = f32[6144,64]{0,1:T(8,128)} async-done(((f32[6144,2048]{0,1:T(8,128)}), f32[6144,64]{0,1:T(8,128)}) %reduce-scatter.26.cloned.1.call-update) | async-done | bytes 1572880 | tf_op jit(solution)/shard_map/reduce_scatter | solution.py:259
  3443.5 438.5 %reduce-scatter.22.cloned.1.call-done = f32[64,6144]{1,0:T(8,128)} async-done(((f32[2048,6144]{1,0:T(8,128)}), f32[64,6144]{1,0:T(8,128)}) %reduce-scatter.22.cloned.1.call-update) | async-done | bytes 1572880 | tf_op jit(solution)/shard_map/reduce_scatter | solution.py:257
  3882.0 438.6 %reduce-scatter.24.cloned.1.call-done = f32[64,6144]{1,0:T(8,128)} async-done(((f32[2048,6144]{1,0:T(8,128)}), f32[64,6144]{1,0:T(8,128)}) %reduce-scatter.24.cloned.1.call-update) | async-done | bytes 1572880 | tf_op jit(solution)/shard_map/reduce_scatter | solution.py:258
  (589 shorter events, 602.6 us)
Async XLA Ops:
  7.2 117.8 %all-gather.12.cloned.1.call-start = ((), (), s32[]{:S(2)}) async-start(), calls=%async_computation.10 | async-start | bytes 10813440 | tf_op jit(solution)/shard_map/all_gather | solution.py:78
  7.9 148.5 %all-gather.14.cloned.1.call-start = ((), (), s32[]{:S(2)}) async-start(), calls=%async_computation.11 | async-start | bytes 1351680 | tf_op jit(solution)/shard_map/all_gather | solution.py:81
  8.7 203.9 %all-gather.16.cloned.1.call-start = ((), (), s32[]{:S(2)}) async-start(), calls=%async_computation.12 | async-start | bytes 1351680 | tf_op jit(solution)/shard_map/all_gather | solution.py:83
  9.4 444.3 %all-gather.10.cloned.1.call-start = ((), (), s32[]{:S(2)}) async-start(), calls=%async_computation.9 | async-start | bytes 10813440 | tf_op jit(solution)/shard_map/all_gather | solution.py:77
  10.0 452.9 %all-gather.18.cloned.1.call-start = ((), (), s32[]{:S(2)}) async-start(), calls=%async_computation.13 | async-start | bytes 10813440 | tf_op jit(solution)/shard_map/all_gather | solution.py:86
  10.7 534.9 %all-gather.20.cloned.1.call-start = ((), (), s32[]{:S(2)}) async-start(), calls=%async_computation.14 | async-start | bytes 25952256 | tf_op jit(solution)/shard_map/all_gather | solution.py:88
  11.2 690.0 %all-gather.22.cloned.1.call-start = ((), (), s32[]{:S(2)}) async-start(), calls=%async_computation.15 | async-start | bytes 25952256 | tf_op jit(solution)/shard_map/all_gather | solution.py:89
  12.0 845.0 %all-gather.24.cloned.1.call-start = ((), (), s32[]{:S(2)}) async-start(), calls=%async_computation.16 | async-start | bytes 25952256 | tf_op jit(solution)/shard_map/all_gather | solution.py:90
  12.7 1390.4 %reduce-scatter.28.cloned.1.call-start = ((), (), s32[]{:S(2)}) async-start(), calls=%async_computation.25 | async-start | bytes 1351680
  420.6 3.2 collective-permute-start
  423.9 3.8 collective-permute-start
  427.7 5.0 collective-permute-start
  432.7 5.2 collective-permute-start
  437.9 5.2 collective-permute-start
  443.1 5.2 collective-permute-start
  448.4 5.2 collective-permute-start
  1123.9 3.1 collective-permute-start.1
  1127.0 4.3 collective-permute-start.1
  1131.4 5.0 collective-permute-start.1
  1136.4 5.0 collective-permute-start.1
  1141.4 5.0 collective-permute-start.1
  1146.4 5.0 collective-permute-start.1
  1151.4 5.1 collective-permute-start.1
  1225.4 281.6 %reduce-scatter.16.cloned.1.call-start = ((), (), s32[]{:S(2)}) async-start(), calls=%async_computation.19 | async-start | bytes 2703360 | tf_op jit(solution)/shard_map/reduce_scatter | solution.py:250
  1227.5 421.0 %reduce-scatter.18.cloned.1.call-start = ((), (), s32[]{:S(2)}) async-start(), calls=%async_computation.20 | async-start | bytes 2703360 | tf_op jit(solution)/shard_map/reduce_scatter | solution.py:252
  1230.5 869.7 %reduce-scatter.20.cloned.1.call-start = ((), (), s32[]{:S(2)}) async-start(), calls=%async_computation.21 | async-start | bytes 21626880 | tf_op jit(solution)/shard_map/reduce_scatter | solution.py:255
  1240.6 1312.1 %reduce-scatter.12.cloned.1.call-start = ((), (), s32[]{:S(2)}) async-start(), calls=%async_computation.17 | async-start | bytes 21626880 | tf_op jit(solution)/shard_map/reduce_scatter | solution.py:246
  1250.4 1754.6 %reduce-scatter.14.cloned.1.call-start = ((), (), s32[]{:S(2)}) async-start(), calls=%async_computation.18 | async-start | bytes 21626880 | tf_op jit(solution)/shard_map/reduce_scatter | solution.py:247
  1252.4 5.9 collective-permute-start.3
  1267.2 2176.3 %reduce-scatter.26.cloned.1.call-start = ((), (), s32[]{:S(2)}) async-start(), calls=%async_computation.24 | async-start | bytes 51904512 | tf_op jit(solution)/shard_map/reduce_scatter | solution.py:259
  1289.1 2592.9 %reduce-scatter.22.cloned.1.call-start = ((), (), s32[]{:S(2)}) async-start(), calls=%async_computation.22 | async-start | bytes 51904512 | tf_op jit(solution)/shard_map/reduce_scatter | solution.py:257
  1311.0 3009.6 %reduce-scatter.24.cloned.1.call-start = ((), (), s32[]{:S(2)}) async-start(), calls=%async_computation.23 | async-start | bytes 51904512 | tf_op jit(solution)/shard_map/reduce_scatter | solution.py:258
  (103 other events, 1437.2 us)
Sparse Core Ops, SparseCore 0:
  10.9 89.6 all-gather.11
  103.4 52.9 all-gather.13
  159.3 53.3 all-gather.15
  215.3 85.7 all-gather.9
  303.8 85.2 all-gather.17
  391.9 153.5 all-gather.19
  548.4 152.8 all-gather.21
  704.1 152.8 all-gather.23
  1225.5 140.8 reduce-scatter.27
  1369.2 137.8 reduce-scatter.15
  1510.0 138.4 reduce-scatter.17
  1651.3 448.9 reduce-scatter.19
  2103.3 449.4 reduce-scatter.11
  2555.6 449.4 reduce-scatter.13
  3013.0 430.3 reduce-scatter.25
  3451.5 430.4 reduce-scatter.21
  3890.0 430.5 reduce-scatter.23
